TPU v7x, 32 devices: a whole 2x2x4 slice. The times are simulated.
32 devices in a mesh: tm: 16 (over z, x, core), comp: 2 (over y).
Axes of the slice: x: 2, y: 2, z: 4, core: 2. Of those that a mesh axis runs over, the one named last changes fastest.
Arguments:
- velocities: bfloat16 [4096, 3, 1024], P('tm', None, 'comp'), may hold values from -6 to 6
- atom_mask: int32 [1024], P('comp'), may hold values 0 or 1
- valid_frames: int32 [1], replicated, may hold values from 3840 to 4096
Outputs:
- correlation: float32 [256, 1024], P('tm', 'comp')
- average: float32 [256], P('tm')
All inputs are finite; a program needn't handle non-finite values. No bound on the sum of `atom_mask` on one device may be relied on, other than what follows from the above.
Results may differ from a plain program's by a relative error of at most 0.0003.
Values may be sent and summed in bfloat16 or wider, within the bound.
A program may use at most 64 MiB of HBM per device.

v0:
```python
import jax
import jax.numpy as jnp
from jax import lax
from jax.sharding import PartitionSpec as P

LAGS = 256


def passed_along(value, axis, steps):
    count = lax.axis_size(axis)
    first, last = (max(0, -steps), min(count, count - steps))
    return lax.ppermute(value, axis, [(source, source + steps) for source in range(first, last)])


def body(velocities, atom_mask, valid_frames):
    frame_count, xyz_count, atom_count = velocities.shape
    last_valid = valid_frames[0]
    anchor_frame = lax.axis_index("tm") * frame_count
    in_range = anchor_frame + jnp.arange(frame_count, dtype=jnp.int32) < last_valid
    clean = jnp.where(in_range[:, None, None], velocities, jnp.zeros_like(velocities))
    leading = clean[: LAGS - 1]
    following = passed_along(leading, "tm", -1)
    extended = jnp.concatenate(
        [clean, following, jnp.zeros((1, xyz_count, atom_count), clean.dtype)], 0
    )
    lag_group = 16
    clean_wide = clean.astype(jnp.float32)

    def block(block_index, lag_sums):
        for member in range(lag_group):
            offset = block_index * lag_group + member
            shifted = lax.dynamic_slice_in_dim(extended, offset, frame_count, 0)
            row_sum = jnp.sum(clean_wide * shifted.astype(jnp.float32), axis=(0, 1))
            lag_sums = lax.dynamic_update_slice_in_dim(lag_sums, row_sum[None, :], offset, 0)
        return lag_sums

    lag_sums = lax.fori_loop(
        0, LAGS // lag_group, block, jnp.zeros((LAGS, atom_count), jnp.float32)
    )
    per_device = LAGS // lax.axis_size("tm")
    first_lag = lax.axis_index("tm") * per_device
    own_rows = lax.psum_scatter(lag_sums, "tm", scatter_dimension=0, tiled=True)
    lag_index = first_lag + jnp.arange(per_device, dtype=jnp.int32)
    anchors = (last_valid - lag_index).astype(jnp.float32)
    atom_weight = atom_mask.astype(jnp.float32)
    correlation = atom_weight[None, :] * own_rows / anchors[:, None]
    total_corr, real_atoms = lax.psum((jnp.sum(correlation, axis=1), jnp.sum(atom_weight)), "comp")
    average = total_corr / jnp.maximum(real_atoms, 1.0)
    return (correlation, average)


def solution(mesh):
    return jax.shard_map(
        body,
        mesh=mesh,
        in_specs=(P("tm", None, "comp"), P("comp"), P()),
        out_specs=(P("tm", "comp"), P("tm")),
        check_vma=False,
    )
```

profile of v0, /device:TPU:0, one launch (start us, length us, event | category | flops | bytes accessed | tf_op | source)
XLA Modules:
  0.0 296.1 jit_solution(7311803472498393615)
XLA Ops:
  7.9 1.3 broadcast_select_fusion
  9.1 1.3 collective-permute-start
  10.4 2.0 copy.7
  13.6 1.4 copy.6
  15.1 197.5 %while.15 = (s32[]{:T(128)}, f32[256,512]{1,0:T(8,128)S(1)}, bf16[512,3,512]{2,1,0:T(4,128)(2,1)S(1)}, f32[256,3,512]{2,1,0:T(4,128)}, s32[]{:T(128)}, /*index=5...) while((s32[]{:T(128)}, f32[256,512]{1,0:T(8,128)S(1)}, ...), condition=%wide.region_17.18_spmd, body=%wide.region_0.17_spmd.sunk | while | flops 18866240 | bytes 14255789 | solution.py:37
  15.2 11.0 %multiply_reduce_fusion.17 = (f32[512]{0:T(512)S(1)}, f32[512]{0:T(512)S(1)}, f32[512]{0:T(512)S(1)}, f32[512]{0:T(512)S(1)}, f32[512]{0:T(512)S(1)}, /*index=5*...) fusion(f32[256,3,512]{2,1,0:T(4,128)} %get-tuple-element.340, ...), kind=kLoop, calls=%fused_computation.clone.1 | loop fusion | flops 18866176 | bytes 14188608 | tf_op jit(solution)/shard_map/while/body/eval_jaxpr/reduce_sum | solution.py:33
  27.6 11.0 %multiply_reduce_fusion.17 = (f32[512]{0:T(512)S(1)}, f32[512]{0:T(512)S(1)}, f32[512]{0:T(512)S(1)}, f32[512]{0:T(512)S(1)}, f32[512]{0:T(512)S(1)}, /*index=5*...) fusion(f32[256,3,512]{2,1,0:T(4,128)} %get-tuple-element.340, ...), kind=kLoop, calls=%fused_computation.clone.1 | loop fusion | flops 18866176 | bytes 14188608 | tf_op jit(solution)/shard_map/while/body/eval_jaxpr/reduce_sum | solution.py:33
  39.9 11.0 %multiply_reduce_fusion.17 = (f32[512]{0:T(512)S(1)}, f32[512]{0:T(512)S(1)}, f32[512]{0:T(512)S(1)}, f32[512]{0:T(512)S(1)}, f32[512]{0:T(512)S(1)}, /*index=5*...) fusion(f32[256,3,512]{2,1,0:T(4,128)} %get-tuple-element.340, ...), kind=kLoop, calls=%fused_computation.clone.1 | loop fusion | flops 18866176 | bytes 14188608 | tf_op jit(solution)/shard_map/while/body/eval_jaxpr/reduce_sum | solution.py:33
  52.2 11.0 %multiply_reduce_fusion.17 = (f32[512]{0:T(512)S(1)}, f32[512]{0:T(512)S(1)}, f32[512]{0:T(512)S(1)}, f32[512]{0:T(512)S(1)}, f32[512]{0:T(512)S(1)}, /*index=5*...) fusion(f32[256,3,512]{2,1,0:T(4,128)} %get-tuple-element.340, ...), kind=kLoop, calls=%fused_computation.clone.1 | loop fusion | flops 18866176 | bytes 14188608 | tf_op jit(solution)/shard_map/while/body/eval_jaxpr/reduce_sum | solution.py:33
  64.6 11.0 %multiply_reduce_fusion.17 = (f32[512]{0:T(512)S(1)}, f32[512]{0:T(512)S(1)}, f32[512]{0:T(512)S(1)}, f32[512]{0:T(512)S(1)}, f32[512]{0:T(512)S(1)}, /*index=5*...) fusion(f32[256,3,512]{2,1,0:T(4,128)} %get-tuple-element.340, ...), kind=kLoop, calls=%fused_computation.clone.1 | loop fusion | flops 18866176 | bytes 14188608 | tf_op jit(solution)/shard_map/while/body/eval_jaxpr/reduce_sum | solution.py:33
  76.9 11.0 %multiply_reduce_fusion.17 = (f32[512]{0:T(512)S(1)}, f32[512]{0:T(512)S(1)}, f32[512]{0:T(512)S(1)}, f32[512]{0:T(512)S(1)}, f32[512]{0:T(512)S(1)}, /*index=5*...) fusion(f32[256,3,512]{2,1,0:T(4,128)} %get-tuple-element.340, ...), kind=kLoop, calls=%fused_computation.clone.1 | loop fusion | flops 18866176 | bytes 14188608 | tf_op jit(solution)/shard_map/while/body/eval_jaxpr/reduce_sum | solution.py:33
  89.3 11.0 %multiply_reduce_fusion.17 = (f32[512]{0:T(512)S(1)}, f32[512]{0:T(512)S(1)}, f32[512]{0:T(512)S(1)}, f32[512]{0:T(512)S(1)}, f32[512]{0:T(512)S(1)}, /*index=5*...) fusion(f32[256,3,512]{2,1,0:T(4,128)} %get-tuple-element.340, ...), kind=kLoop, calls=%fused_computation.clone.1 | loop fusion | flops 18866176 | bytes 14188608 | tf_op jit(solution)/shard_map/while/body/eval_jaxpr/reduce_sum | solution.py:33
  101.6 11.0 %multiply_reduce_fusion.17 = (f32[512]{0:T(512)S(1)}, f32[512]{0:T(512)S(1)}, f32[512]{0:T(512)S(1)}, f32[512]{0:T(512)S(1)}, f32[512]{0:T(512)S(1)}, /*index=5*...) fusion(f32[256,3,512]{2,1,0:T(4,128)} %get-tuple-element.340, ...), kind=kLoop, calls=%fused_computation.clone.1 | loop fusion | flops 18866176 | bytes 14188608 | tf_op jit(solution)/shard_map/while/body/eval_jaxpr/reduce_sum | solution.py:33
  114.0 11.0 %multiply_reduce_fusion.17 = (f32[512]{0:T(512)S(1)}, f32[512]{0:T(512)S(1)}, f32[512]{0:T(512)S(1)}, f32[512]{0:T(512)S(1)}, f32[512]{0:T(512)S(1)}, /*index=5*...) fusion(f32[256,3,512]{2,1,0:T(4,128)} %get-tuple-element.340, ...), kind=kLoop, calls=%fused_computation.clone.1 | loop fusion | flops 18866176 | bytes 14188608 | tf_op jit(solution)/shard_map/while/body/eval_jaxpr/reduce_sum | solution.py:33
  126.3 11.0 %multiply_reduce_fusion.17 = (f32[512]{0:T(512)S(1)}, f32[512]{0:T(512)S(1)}, f32[512]{0:T(512)S(1)}, f32[512]{0:T(512)S(1)}, f32[512]{0:T(512)S(1)}, /*index=5*...) fusion(f32[256,3,512]{2,1,0:T(4,128)} %get-tuple-element.340, ...), kind=kLoop, calls=%fused_computation.clone.1 | loop fusion | flops 18866176 | bytes 14188608 | tf_op jit(solution)/shard_map/while/body/eval_jaxpr/reduce_sum | solution.py:33
  138.7 11.0 %multiply_reduce_fusion.17 = (f32[512]{0:T(512)S(1)}, f32[512]{0:T(512)S(1)}, f32[512]{0:T(512)S(1)}, f32[512]{0:T(512)S(1)}, f32[512]{0:T(512)S(1)}, /*index=5*...) fusion(f32[256,3,512]{2,1,0:T(4,128)} %get-tuple-element.340, ...), kind=kLoop, calls=%fused_computation.clone.1 | loop fusion | flops 18866176 | bytes 14188608 | tf_op jit(solution)/shard_map/while/body/eval_jaxpr/reduce_sum | solution.py:33
  151.0 11.0 %multiply_reduce_fusion.17 = (f32[512]{0:T(512)S(1)}, f32[512]{0:T(512)S(1)}, f32[512]{0:T(512)S(1)}, f32[512]{0:T(512)S(1)}, f32[512]{0:T(512)S(1)}, /*index=5*...) fusion(f32[256,3,512]{2,1,0:T(4,128)} %get-tuple-element.340, ...), kind=kLoop, calls=%fused_computation.clone.1 | loop fusion | flops 18866176 | bytes 14188608 | tf_op jit(solution)/shard_map/while/body/eval_jaxpr/reduce_sum | solution.py:33
  163.3 11.0 %multiply_reduce_fusion.17 = (f32[512]{0:T(512)S(1)}, f32[512]{0:T(512)S(1)}, f32[512]{0:T(512)S(1)}, f32[512]{0:T(512)S(1)}, f32[512]{0:T(512)S(1)}, /*index=5*...) fusion(f32[256,3,512]{2,1,0:T(4,128)} %get-tuple-element.340, ...), kind=kLoop, calls=%fused_computation.clone.1 | loop fusion | flops 18866176 | bytes 14188608 | tf_op jit(solution)/shard_map/while/body/eval_jaxpr/reduce_sum | solution.py:33
  175.7 11.0 %multiply_reduce_fusion.17 = (f32[512]{0:T(512)S(1)}, f32[512]{0:T(512)S(1)}, f32[512]{0:T(512)S(1)}, f32[512]{0:T(512)S(1)}, f32[512]{0:T(512)S(1)}, /*index=5*...) fusion(f32[256,3,512]{2,1,0:T(4,128)} %get-tuple-element.340, ...), kind=kLoop, calls=%fused_computation.clone.1 | loop fusion | flops 18866176 | bytes 14188608 | tf_op jit(solution)/shard_map/while/body/eval_jaxpr/reduce_sum | solution.py:33
  188.0 11.0 %multiply_reduce_fusion.17 = (f32[512]{0:T(512)S(1)}, f32[512]{0:T(512)S(1)}, f32[512]{0:T(512)S(1)}, f32[512]{0:T(512)S(1)}, f32[512]{0:T(512)S(1)}, /*index=5*...) fusion(f32[256,3,512]{2,1,0:T(4,128)} %get-tuple-element.340, ...), kind=kLoop, calls=%fused_computation.clone.1 | loop fusion | flops 18866176 | bytes 14188608 | tf_op jit(solution)/shard_map/while/body/eval_jaxpr/reduce_sum | solution.py:33
  200.4 11.0 %multiply_reduce_fusion.17 = (f32[512]{0:T(512)S(1)}, f32[512]{0:T(512)S(1)}, f32[512]{0:T(512)S(1)}, f32[512]{0:T(512)S(1)}, f32[512]{0:T(512)S(1)}, /*index=5*...) fusion(f32[256,3,512]{2,1,0:T(4,128)} %get-tuple-element.340, ...), kind=kLoop, calls=%fused_computation.clone.1 | loop fusion | flops 18866176 | bytes 14188608 | tf_op jit(solution)/shard_map/while/body/eval_jaxpr/reduce_sum | solution.py:33
  214.0 66.9 %reduce-scatter.2.cloned.1.call-done = f32[16,512]{1,0:T(8,128)} async-done(((f32[256,512]{1,0:T(8,128)}), f32[16,512]{1,0:T(8,128)}) %reduce-scatter.2.cloned.1.call-update) | async-done | bytes 32784 | tf_op jit(solution)/shard_map/reduce_scatter | solution.py:42
  281.0 1.6 fusion
  282.5 5.6 %all-reduce = (f32[16]{0:T(128)S(1)}, f32[]{:T(128)}) all-reduce(f32[16]{0:T(128)S(1)} %get-tuple-element.172, f32[]{:T(128)} %convert_reduce_fusion), channel_id=1, replica_groups=mesh['tm'=16,'comp'=2] {'comp'}, use_global_device_ids=true, to_apply=%region_20.21 | all-reduce | flops 17 | bytes 136 | tf_op jit(solution)/shard_map/psum | solution.py:47
  (271 shorter events, 18.8 us)
Async XLA Ops:
  7.2 273.8 %reduce-scatter.2.cloned.1.call-start = ((), (), s32[]{:S(2)}) async-start(), calls=%async_computation.1 | async-start | bytes 557056 | tf_op jit(solution)/shard_map/reduce_scatter | solution.py:42
  9.1 4.2 %collective-permute-start = (bf16[255,3,512]{2,0,1:T(8,128)(2,1)S(1)}, bf16[255,3,512]{2,0,1:T(8,128)(2,1)S(1)}, u32[]{:S(2)}, u32[]{:S(2)}) collective-permute-start(bf16[255,3,512]{2,0,1:T(8,128)(2,1)S(1)} %bitcast.53), channel_id=1, source_target_pairs={{2,0},{4,2},{6,4},{8,6},{10,8},{12,10},{14,12},{16,14},{18,16},{20... | collective-permute-start | bytes 2350088 | tf_op jit(solution)/shard_map/ppermute | solution.py:12
  15.1 198.3 %copy-start.1 = (s32[512]{0:T(512)S(1)}, s32[512]{0:T(512)}, u32[]{:S(2)}) copy-start(s32[512]{0:T(512)} %param.6) | copy-start | bytes 6148
  212.6 0.8 copy-start
Sparse Core Ops, SparseCore 0:
  213.5 67.4 reduce-scatter.1
where the time goes:
time: 297 us; the launch traced here: 296 us
  other arithmetic  179 us (60%)
  waiting for transfers between devices  67.7 us (23%)
  local copies, waits for them, and re-layouts  19.9 us (7%)
  between operations  15.4 us (5%)
  loops' own time  6.67 us (2%)
  blocking collectives  5.56 us (2%)
    reduce_sum x16, other arithmetic, block(): row_sum = jnp.sum(clean_wide * shifted.astype(jnp.float32), axis=(0, 1))  175 us
    reduce_scatter x1, waiting for transfers between devices, body(): own_rows = lax.psum_scatter(lag_sums, 'tm', scatter_dimension=0, tiled=True)  66.9 us
    dynamic_update_slice x256, local copies, waits for them, and re-layouts, block(): lax.dynamic_update_slice_in_dim(lag_sums, row_sum[None, :], offset, 0)  15.6 us
    another operation x1, loops' own time, body(): lax.fori_loop(0, LAGS // lag_group, block, jnp.zeros((LAGS, atom_count),...  6.67 us
  transfers between devices with their start and end apart: 2, of which 2 were waited for; matrix products, arithmetic and copies ran while one was open for 1% of the time, Pallas kernels for 0%

commit v1 on v0

v1 whole, which is shorter than its diff:
```python
import functools
import math

import jax
import jax.numpy as jnp
import numpy as np
from jax import lax
from jax.sharding import PartitionSpec as P

LAGS = 256


def split_bf16(table):
    high = table.astype(np.float32).astype(jnp.bfloat16)
    low = (table - high.astype(np.float64)).astype(np.float32).astype(jnp.bfloat16)
    return high, low


@functools.lru_cache
def tables(frame_count):
    length = 2 * frame_count
    bins = np.arange(frame_count, dtype=np.int64)[:, None]
    own = np.arange(frame_count, dtype=np.int64)[None, :]
    angle = (((2 * bins + 1) * own) % (2 * length)) * (math.pi / length)
    forward = np.concatenate([np.cos(angle), np.sin(angle)], 0)
    lags = np.arange(LAGS, dtype=np.int64)[:, None]
    angle = (((2 * bins.T + 1) * lags) % (2 * length)) * (math.pi / length)
    inverse = np.concatenate([np.cos(angle), -np.sin(angle)], 1) * (2.0 / length)
    sign = np.where(bins % 2 == 0, 1.0, -1.0).astype(np.float32)
    return split_bf16(forward), split_bf16(inverse), sign


def dot(a, b):
    return jnp.dot(a, b, preferred_element_type=jnp.float32)


def body(velocities, atom_mask, valid_frames):
    frame_count, xyz_count, atom_count = velocities.shape
    last_valid = valid_frames[0]
    count = lax.axis_size("tm")
    following = lax.ppermute(velocities, "tm", [(s, s - 1) for s in range(1, count)])
    anchor_frame = lax.axis_index("tm") * frame_count
    frame = anchor_frame + jnp.arange(frame_count, dtype=jnp.int32)
    (fwd_hi, fwd_lo), (inv_hi, inv_lo), sign = tables(frame_count)

    def spectrum(block, frames, k):
        x = jnp.where((frames < last_valid)[:, None], block[:, k, :], jnp.zeros((), block.dtype))
        y = dot(fwd_hi, x) + dot(fwd_lo, x)
        return y[:frame_count], y[frame_count:]

    real = imag = 0.0
    for k in range(xyz_count):
        ac, as_ = spectrum(velocities, frame, k)
        nc, ns = spectrum(following, frame + frame_count, k)
        nc, ns = -sign * ns, sign * nc
        real = real + ac * (ac + nc) + as_ * (as_ + ns)
        imag = imag + as_ * nc - ac * ns
    power = jnp.concatenate([real, imag], 0)
    rounded = lax.reduce_precision(power, 8, 7)
    p_hi = rounded.astype(jnp.bfloat16)
    p_lo = (power - rounded).astype(jnp.bfloat16)
    lag_sums = dot(inv_hi, p_hi) + (dot(inv_hi, p_lo) + dot(inv_lo, p_hi))

    per_device = LAGS // count
    first_lag = lax.axis_index("tm") * per_device
    own_rows = lax.psum_scatter(lag_sums, "tm", scatter_dimension=0, tiled=True)
    lag_index = first_lag + jnp.arange(per_device, dtype=jnp.int32)
    anchors = (last_valid - lag_index).astype(jnp.float32)
    atom_weight = atom_mask.astype(jnp.float32)
    correlation = atom_weight[None, :] * own_rows / anchors[:, None]
    total_corr, real_atoms = lax.psum((jnp.sum(correlation, axis=1), jnp.sum(atom_weight)), "comp")
    average = total_corr / jnp.maximum(real_atoms, 1.0)
    return (correlation, average)


def solution(mesh):
    return jax.shard_map(
        body,
        mesh=mesh,
        in_specs=(P("tm", None, "comp"), P("comp"), P()),
        out_specs=(P("tm", "comp"), P("tm")),
        check_vma=False,
    )
```

time: 297 us -> 101 us (0.34)
  other arithmetic: 179 us -> 2.1 us
  local copies, waits for them, and re-layouts: 19.9 us -> 5.21 us
  loops' own time: 6.67 us -> 0 us
  matrix products: 0 us -> 6.59 us
  waiting for transfers between devices: 67.7 us -> 64.7 us
    reduce_sum x16 -> x0, other arithmetic: 175 us -> none  [block(): row_sum = jnp.sum(clean_wide * shifted.astype(jnp.float32), axis=(0, 1))]
    reduce_scatter x1 -> x0, waiting for transfers between devices: 66.9 us -> none  [body(): own_rows = lax.psum_scatter(lag_sums, 'tm', scatter_dimension=0, tiled=True)]
    unnamed x1 -> x2, waiting for transfers between devices: 0.02 us -> 64.7 us
    dynamic_update_slice x256 -> x0, local copies, waits for them, and re-layouts: 15.6 us -> none  [block(): lax.dynamic_update_slice_in_dim(lag_sums, row_sum[None, :], offset, 0)]
    another operation x1 -> x0, loops' own time: 6.67 us -> none  [body(): lax.fori_loop(0, LAGS // lag_group, block, jnp.zeros((LAGS, atom_count),...]
    dot_general x0 -> x15, matrix products: none -> 6.59 us  [dot(): return jnp.dot(a, b, preferred_element_type=jnp.float32)]
    unnamed x4 -> x19, local copies, waits for them, and re-layouts: 0.79 us -> 5.21 us
    while x2 -> x0, local copies, waits for them, and re-layouts: 3.38 us -> none  [body(): lax.fori_loop(0, LAGS // lag_group, block, jnp.zeros((LAGS, atom_count),...]
  transfers between devices with their start and end apart: 2 -> 2, of which waited for: 2 -> 1; matrix products, arithmetic and copies ran while one was open for 1% -> 4% of each run, Pallas kernels for 0% -> 0%
where the time goes in v1:
time: 101 us
  waiting for transfers between devices  64.7 us (64%)
  between operations  15.5 us (15%)
  matrix products  6.59 us (7%)
  blocking collectives  5.54 us (5%)
  local copies, waits for them, and re-layouts  5.21 us (5%)
  other arithmetic  2.1 us (2%)
  starting transfers between devices  1.33 us (1%)
    unnamed x2, waiting for transfers between devices  64.7 us
    dot_general x15, matrix products, dot(): return jnp.dot(a, b, preferred_element_type=jnp.float32)  6.59 us
    psum x1, blocking collectives, body(): lax.psum((jnp.sum(correlation, axis=1), jnp.sum(atom_weight)), 'comp')  5.54 us
    unnamed x19, local copies, waits for them, and re-layouts  5.21 us
  transfers between devices with their start and end apart: 2, of which 1 were waited for; matrix products, arithmetic and copies ran while one was open for 4% of the time, Pallas kernels for 0%

profile of v1, /device:TPU:0, one launch (start us, length us, event | category | flops | bytes accessed | tf_op | source)
XLA Modules:
  0.0 101.0 jit_solution(7385749034053999529)
XLA Ops:
  7.2 1.3 %collective-permute-start = (bf16[256,3,512]{2,0,1:T(8,128)(2,1)}, bf16[256,3,512]{2,0,1:T(8,128)(2,1)S(1)}, u32[]{:S(2)}, u32[]{:S(2)}) collective-permute-start(bf16[256,3,512]{2,0,1:T(8,128)(2,1)} %param.11), channel_id=1, source_target_pairs={{2,0},{4,2},{6,4},{8,6},{10,8},{12,10},{14,12},{16,14},{18,16},{20... | collective-permute-start | bytes 2359304 | tf_op jit(solution)/shard_map/ppermute | solution.py:41
  9.2 1.5 %fusion.21 = f32[512,512]{0,1:T(8,128)S(1)} fusion(bf16[512,256]{1,0:T(8,128)(2,1)} %constant.29.clone, bf16[256,3,512]{2,0,1:T(8,128)(2,1)} %param.11, pred[256]{0:T(512)(128)(4,1)S(1)} %get-tuple-element.11), kind=kOutput, calls=%fused_computation.50 | convolution fusion | flops 134348800 | bytes 1573120 | tf_op jit(solution)/shard_map/dot_general | solution.py:34
  10.7 0.4 fusion.20
  11.1 0.6 copy-done.1
  11.7 0.4 fusion.1
  12.0 0.4 fusion.19
  12.4 0.4 fusion.3
  12.8 0.4 fusion.5
  13.5 0.4 fusion.26
  13.9 0.4 fusion.29
  14.3 0.4 fusion.4
  14.7 0.4 fusion.2
  15.1 0.4 fusion
  16.1 0.5 fusion.13
  16.6 0.5 copy-done.3
  17.8 0.6 copy-done.4
  18.7 1.0 copy.15
  19.8 0.7 copy-done.5
  20.4 0.6 convert_reduce_fusion
  21.0 64.7 %reduce-scatter.4.cloned.1.call-done = f32[16,512]{1,0:T(8,128)} async-done(((f32[256,512]{1,0:T(8,128)}), f32[16,512]{1,0:T(8,128)}) %reduce-scatter.4.cloned.1.call-update) | async-done | bytes 32784
  85.7 0.9 copy.16
  86.8 0.7 copy.14
  87.5 5.5 %all-reduce = (f32[16]{0:T(128)S(1)}, f32[]{:T(128)}) all-reduce(f32[16]{0:T(128)S(1)} %get-tuple-element.8, f32[]{:T(128)} %convert_reduce_fusion), channel_id=1, replica_groups=mesh['tm'=16,'comp'=2] {'comp'}, use_global_device_ids=true, to_apply=%region_2.3 | all-reduce | flops 17 | bytes 136 | tf_op jit(solution)/shard_map/psum | solution.py:71
  93.7 0.5 broadcast_divide_fusion
  (24 shorter events, 2.3 us)
Async XLA Ops:
  7.2 78.6 %reduce-scatter.4.cloned.1.call-start = ((), (), s32[]{:S(2)}) async-start(), calls=%async_computation.1 | async-start | bytes 557056
  7.2 6.0 %collective-permute-start = (bf16[256,3,512]{2,0,1:T(8,128)(2,1)}, bf16[256,3,512]{2,0,1:T(8,128)(2,1)S(1)}, u32[]{:S(2)}, u32[]{:S(2)}) collective-permute-start(bf16[256,3,512]{2,0,1:T(8,128)(2,1)} %param.11), channel_id=1, source_target_pairs={{2,0},{4,2},{6,4},{8,6},{10,8},{12,10},{14,12},{16,14},{18,16},{20... | collective-permute-start | bytes 2359304 | tf_op jit(solution)/shard_map/ppermute | solution.py:41
  9.2 1.5 %copy-start = (bf16[512,256]{1,0:T(8,128)(2,1)S(1)}, bf16[512,256]{1,0:T(8,128)(2,1)}, u32[]{:S(2)}) copy-start(bf16[512,256]{1,0:T(8,128)(2,1)} %constant.29.clone) | copy-start | bytes 786436
  9.2 1.5 %copy-start.2 = (bf16[256,3,512]{2,0,1:T(8,128)(2,1)S(1)}, bf16[256,3,512]{2,0,1:T(8,128)(2,1)}, u32[]{:S(2)}) copy-start(bf16[256,3,512]{2,0,1:T(8,128)(2,1)} %param.11) | copy-start | bytes 2359300
  10.7 1.0 copy-start.1
  15.0 0.7 copy-start.6
  15.0 0.7 copy-start.7
  16.1 1.0 copy-start.3
  17.4 1.0 copy-start.4
  19.7 0.7 copy-start.5
Sparse Core Ops, SparseCore 0:
  19.9 65.8 reduce-scatter.3

commit v2 on v1

v2 whole, which is shorter than its diff:
```python
import functools
import math

import jax
import jax.numpy as jnp
import numpy as np
from jax import lax
from jax.experimental import pallas as pl
from jax.experimental.pallas import tpu as pltpu
from jax.sharding import PartitionSpec as P

LAGS = 256
CHUNKS = 2
MESH = pl.DeviceIdType.MESH


def split_bf16(table):
    high = table.astype(np.float32).astype(jnp.bfloat16)
    low = (table - high.astype(np.float64)).astype(np.float32).astype(jnp.bfloat16)
    return high, low


@functools.lru_cache
def tables(frame_count, count):
    length = 2 * frame_count
    bins = np.arange(frame_count, dtype=np.int64)[:, None]
    own = np.arange(frame_count, dtype=np.int64)[None, :]
    angle = (((2 * bins + 1) * own) % (2 * length)) * (math.pi / length)
    forward = np.concatenate([np.cos(angle), np.sin(angle)], 0)
    per = LAGS // count
    lags = np.arange(LAGS, dtype=np.int64).reshape(count // 4, 2, 2, per)
    lags = lags.transpose(2, 1, 0, 3).reshape(LAGS, 1)
    angle = (((2 * bins.T + 1) * lags) % (2 * length)) * (math.pi / length)
    inverse = np.concatenate([np.cos(angle), -np.sin(angle)], 1) * (2.0 / length)
    return split_bf16(forward) + split_bf16(inverse)


def dot(a, b):
    return jnp.dot(a, b, preferred_element_type=jnp.float32)


def kernel(
    n, groups,
    valid_ref, vel_ref, mask_ref, fwd_hi, fwd_lo, inv_hi, inv_lo,
    corr_ref, avg_ref,
    nxt, spec, part, pair_in, q_ref, x_in, r_ref, z_in, comp_out, comp_in,
    halo_s, halo_r, pair_s, pair_r, x_s, x_r, z_s, z_r, comp_s, comp_r,
):
    xyz, frames, atoms = vel_ref.shape
    width = atoms // CHUNKS
    nz = n // 4
    per = LAGS // n
    me = lax.axis_index("tm")
    mine = lax.axis_index("comp")
    core = lax.rem(me, 2)
    xpos = lax.rem(me // 2, 2)
    zpos = me // 4
    pair = me + 1 - 2 * core
    across = me + 2 - 4 * xpos
    left = lax.rem(me + n - 1, n)
    right = lax.rem(me + 1, n)

    def along_z(d):
        return lax.rem(zpos + d, nz)

    def z_device(d):
        return along_z(d) * 4 + lax.rem(me, 4)

    barrier = pltpu.get_barrier_semaphore()
    for device in [left, right, pair, across] + [z_device(d) for d in range(1, nz)]:
        pl.semaphore_signal(barrier, inc=1, device_id={"tm": device}, device_id_type=MESH)
    for d in range(1, groups):
        pl.semaphore_signal(
            barrier, inc=1, device_id={"comp": lax.rem(mine + d, groups)}, device_id_type=MESH
        )
    pl.semaphore_wait(barrier, 4 + (nz - 1) + (groups - 1))

    def remote(src, dst, send, recv, device):
        return pltpu.make_async_remote_copy(
            src_ref=src, dst_ref=dst, send_sem=send, recv_sem=recv,
            device_id=device, device_id_type=MESH,
        )

    def halo(c, k):
        lanes = pl.ds(c * width, width)
        return remote(
            vel_ref.at[k, :, lanes], nxt.at[c, k], halo_s.at[c, k], halo_r.at[c, k], {"tm": left}
        )

    @pl.when(me > 0)
    def _():
        for c in range(CHUNKS):
            for k in range(xyz):
                halo(c, k).start()

    @pl.when(me == n - 1)
    def _():
        nxt[...] = jnp.zeros_like(nxt)

    last_valid = valid_ref[0]
    row = lax.broadcasted_iota(jnp.int32, (frames, width), 0) + me * frames
    keep_own = jnp.where(row < last_valid, 1.0, 0.0).astype(jnp.bfloat16)
    keep_nxt = jnp.where(row + frames < last_valid, 1.0, 0.0).astype(jnp.bfloat16)
    bins = lax.broadcasted_iota(jnp.int32, (frames, width), 0)
    sign = jnp.where(lax.rem(bins, 2) == 0, 1.0, -1.0)

    def spectrum(x):
        return dot(fwd_hi[...], x) + dot(fwd_lo[...], x)

    for c in range(CHUNKS):
        for k in range(xyz):
            spec[c, k] = spectrum(vel_ref[k, :, c * width : (c + 1) * width] * keep_own)

    def pair_copy(c):
        return remote(part.at[c, 1 - core], pair_in.at[c], pair_s.at[c], pair_r.at[c], {"tm": pair})

    def x_copy(c):
        return remote(q_ref.at[c, 1 - xpos], x_in.at[c], x_s.at[c], x_r.at[c], {"tm": across})

    def z_copy(c, d):
        return remote(
            r_ref.at[c, along_z(d)], z_in.at[c, d - 1], z_s.at[c, d - 1], z_r.at[c, d - 1],
            {"tm": z_device(d)},
        )

    def correlate(c):
        real = imag = 0.0
        for k in range(xyz):
            @pl.when(me < n - 1)
            def _():
                halo(c, k).wait_recv()

            other = spectrum(nxt[c, k] * keep_nxt)
            nc, ns = -sign * other[frames:], sign * other[:frames]
            ac, as_ = spec[c, k, :frames], spec[c, k, frames:]
            real = real + ac * (ac + nc) + as_ * (as_ + ns)
            imag = imag + as_ * nc - ac * ns
        power = jnp.concatenate([real, imag], 0)
        high = power.astype(jnp.bfloat16)
        low = (power - high.astype(jnp.float32)).astype(jnp.bfloat16)
        sums = dot(inv_hi[...], high) + (dot(inv_hi[...], low) + dot(inv_lo[...], high))
        part[c] = sums.reshape(part.shape[1:])
        pair_copy(c).start()

    def after_pair(c):
        pair_copy(c).wait_recv()
        q_ref[c] = part[c, core] + pair_in[c]
        x_copy(c).start()

    def after_x(c):
        x_copy(c).wait_recv()
        r_ref[c] = q_ref[c, xpos] + x_in[c]
        for d in range(1, nz):
            z_copy(c, d).start()

    correlate(0)
    after_pair(0)
    for c in range(1, CHUNKS):
        correlate(c)
        after_x(c - 1)
        after_pair(c)
    after_x(CHUNKS - 1)

    lag = me * per + lax.broadcasted_iota(jnp.int32, (per, width), 0)
    anchors = (last_valid - lag).astype(jnp.float32)
    weight = mask_ref[...].astype(jnp.float32)
    total = jnp.zeros((per, 1), jnp.float32)
    for c in range(CHUNKS):
        rows = r_ref[c, zpos]
        for d in range(1, nz):
            z_copy(c, d).wait_recv()
            rows = rows + z_in[c, d - 1]
        lanes = slice(c * width, (c + 1) * width)
        corr = weight[:, lanes] * rows / anchors
        corr_ref[:, lanes] = corr
        total = total + jnp.sum(corr, axis=1, keepdims=True)
    real_atoms = jnp.sum(weight, axis=1, keepdims=True)
    comp_out[:per] = jnp.broadcast_to(total, (per, 128))
    comp_out[per:] = jnp.broadcast_to(real_atoms, (8, 128))

    def comp_copy(d):
        return remote(
            comp_out, comp_in.at[d - 1], comp_s.at[d - 1], comp_r.at[d - 1],
            {"comp": lax.rem(mine + d, groups)},
        )

    for d in range(1, groups):
        comp_copy(d).start()
    both = comp_out[...]
    for d in range(1, groups):
        comp_copy(d).wait_recv()
        both = both + comp_in[d - 1]
    avg_ref[...] = both[:per] / jnp.maximum(both[per : per + 1], 1.0)

    @pl.when(me > 0)
    def _():
        for c in range(CHUNKS):
            for k in range(xyz):
                halo(c, k).wait_send()

    for c in range(CHUNKS):
        pair_copy(c).wait_send()
        x_copy(c).wait_send()
        for d in range(1, nz):
            z_copy(c, d).wait_send()
    for d in range(1, groups):
        comp_copy(d).wait_send()


def body(velocities, atom_mask, valid_frames):
    frames, xyz, atoms = velocities.shape
    n = lax.axis_size("tm")
    groups = lax.axis_size("comp")
    nz, per, width = n // 4, LAGS // n, atoms // CHUNKS
    f32 = jnp.float32
    vmem = pl.BlockSpec(memory_space=pltpu.VMEM)
    dma = pltpu.SemaphoreType.DMA
    correlation, average = pl.pallas_call(
        functools.partial(kernel, n, groups),
        out_shape=(
            jax.ShapeDtypeStruct((per, atoms), f32),
            jax.ShapeDtypeStruct((per, 128), f32),
        ),
        in_specs=[pl.BlockSpec(memory_space=pltpu.SMEM)] + [vmem] * 6,
        out_specs=(vmem, vmem),
        scratch_shapes=[
            pltpu.VMEM((CHUNKS, xyz, frames, width), jnp.bfloat16),
            pltpu.VMEM((CHUNKS, xyz, 2 * frames, width), f32),
            pltpu.VMEM((CHUNKS, 2, 2, nz, per, width), f32),
            pltpu.VMEM((CHUNKS, 2, nz, per, width), f32),
            pltpu.VMEM((CHUNKS, 2, nz, per, width), f32),
            pltpu.VMEM((CHUNKS, nz, per, width), f32),
            pltpu.VMEM((CHUNKS, nz, per, width), f32),
            pltpu.VMEM((CHUNKS, nz - 1, per, width), f32),
            pltpu.VMEM((per + 8, 128), f32),
            pltpu.VMEM((groups - 1, per + 8, 128), f32),
            dma((CHUNKS, xyz)), dma((CHUNKS, xyz)),
            dma((CHUNKS,)), dma((CHUNKS,)),
            dma((CHUNKS,)), dma((CHUNKS,)),
            dma((CHUNKS, nz - 1)), dma((CHUNKS, nz - 1)),
            dma((groups - 1,)), dma((groups - 1,)),
        ],
        compiler_params=pltpu.CompilerParams(
            collective_id=0, has_side_effects=True, vmem_limit_bytes=40 * 1024 * 1024
        ),
    )(
        valid_frames, jnp.transpose(velocities, (1, 0, 2)), atom_mask[None, :],
        *tables(frames, n),
    )
    return correlation, average[:, 0]


def solution(mesh):
    return jax.shard_map(
        body,
        mesh=mesh,
        in_specs=(P("tm", None, "comp"), P("comp"), P()),
        out_specs=(P("tm", "comp"), P("tm")),
        check_vma=False,
    )
```

time: 101 us -> 36.4 us (0.36)
  waiting for transfers between devices: 64.7 us -> 0 us
  Pallas kernels: 0 us -> 27.9 us
  between operations: 15.5 us -> 1.3 us
  matrix products: 6.59 us -> 0 us
  blocking collectives: 5.54 us -> 0 us
  other arithmetic: 2.1 us -> 0 us
  local copies, waits for them, and re-layouts: 5.21 us -> 6.85 us
  starting transfers between devices: 1.33 us -> 0 us
    unnamed x2 -> x0, waiting for transfers between devices: 64.7 us -> none
    pallas_call x0 -> x1, Pallas kernels: none -> 27.9 us  [body(): pl.pallas_call(functools.partial(kernel, n, groups), out_shape=(jax.Shape...]
    dot_general x15 -> x0, matrix products: 6.59 us -> none  [dot(): return jnp.dot(a, b, preferred_element_type=jnp.float32)]
    psum x1 -> x0, blocking collectives: 5.54 us -> none  [body(): lax.psum((jnp.sum(correlation, axis=1), jnp.sum(atom_weight)), 'comp')]
    ppermute x1 -> x0, starting transfers between devices: 1.29 us -> none  [body(): lax.ppermute(velocities, 'tm', [(s, s - 1) for s in range(1, count)])]
    unnamed x19 -> x13, local copies, waits for them, and re-layouts: 5.21 us -> 6.22 us
  transfers between devices with their start and end apart: 2 -> 0, of which waited for: 1 -> 0; matrix products, arithmetic and copies ran while one was open for 4% -> 0% of each run, Pallas kernels for 0% -> 0%
where the time goes in v2:
time: 36.4 us; the launch traced here: 36 us
  Pallas kernels  27.9 us (77%)
  local copies, waits for them, and re-layouts  6.85 us (19%)
  between operations  1.3 us (4%)
    pallas_call x1, Pallas kernels, body(): pl.pallas_call(functools.partial(kernel, n, groups), out_shape=(jax.Shape...  27.9 us
    unnamed x13, local copies, waits for them, and re-layouts  6.22 us

profile of v2, /device:TPU:0, one launch (start us, length us, event | category | flops | bytes accessed | tf_op | source)
XLA Modules:
  0.0 36.0 jit_solution(4887995349908536369)
XLA Ops:
  1.3 0.0 copy-start.5
  1.3 0.7 %copy-done.5 = s32[512]{0:T(512)S(1)} copy-done((s32[512]{0:T(512)S(1)}, s32[512]{0:T(512)}, u32[]{:S(2)}) %copy-start.5) | copy-done | bytes 2072
  2.0 0.0 copy-start
  2.0 1.1 %copy-done = bf16[256,3,512]{2,0,1:T(8,128)(2,1)S(1)} copy-done((bf16[256,3,512]{2,0,1:T(8,128)(2,1)S(1)}, bf16[256,3,512]{2,0,1:T(8,128)(2,1)}, u32[]{:S(2)}) %copy-start) | copy-done | bytes 786456
  3.1 0.0 copy-start.1
  3.1 0.9 %copy-done.1 = bf16[256,512]{1,0:T(8,128)(2,1)S(1)} copy-done((bf16[256,512]{1,0:T(8,128)(2,1)S(1)}, bf16[256,512]{1,0:T(8,128)(2,1)}, u32[]{:S(2)}) %copy-start.1) | copy-done | bytes 262168
  4.0 0.0 copy-start.2
  4.0 0.9 %copy-done.2 = bf16[256,512]{1,0:T(8,128)(2,1)S(1)} copy-done((bf16[256,512]{1,0:T(8,128)(2,1)S(1)}, bf16[256,512]{1,0:T(8,128)(2,1)}, u32[]{:S(2)}) %copy-start.2) | copy-done | bytes 262168
  5.0 0.0 copy-start.3
  5.0 0.9 %copy-done.3 = bf16[512,256]{1,0:T(8,128)(2,1)S(1)} copy-done((bf16[512,256]{1,0:T(8,128)(2,1)S(1)}, bf16[512,256]{1,0:T(8,128)(2,1)}, u32[]{:S(2)}) %copy-start.3) | copy-done | bytes 262168
  5.9 0.0 copy-start.4
  5.9 0.9 %copy-done.4 = bf16[512,256]{1,0:T(8,128)(2,1)S(1)} copy-done((bf16[512,256]{1,0:T(8,128)(2,1)S(1)}, bf16[512,256]{1,0:T(8,128)(2,1)}, u32[]{:S(2)}) %copy-start.4) | copy-done | bytes 262168
  6.9 27.9 %shard_map.86 = (f32[16,512]{1,0:T(8,128)S(1)}, f32[16,128]{1,0:T(8,128)S(1)}) custom-call(s32[1]{0:T(128)S(6)} %copy.10.valid_ref, bf16[3,256,512]{2,1,0:T(8,128)(2,1)S(1)} %bitcast.2, s32[1,512]{1,0:T(1,128)S(1)} %bitcast.3, bf16[512,256]{1,0:T(8,128)(2,1)S(1)} %copy-done.4, bf16[512,256]{1,0:T(8,128)(2,1)S(1)} %copy-done.3, ...), custom_call_target="tpu_custom_call" | custom-call | tf_op jit(solution)/shard_map/pallas_call | solution.py:218
  34.8 0.6 %slice_reduce_fusion = f32[16]{0:T(128)} fusion(f32[16,128]{1,0:T(8,128)S(1)} %get-tuple-element.5), kind=kLoop, calls=%fused_computation | loop fusion | bytes 128 | tf_op jit(solution)/shard_map/slice | solution.py:250
  35.4 0.6 %copy.11 = f32[16,512]{1,0:T(8,128)} copy(f32[16,512]{1,0:T(8,128)S(1)} %get-tuple-element.8) | data formatting | bytes 65536
Async XLA Ops:
  1.3 0.7 %copy-start.5 = (s32[512]{0:T(512)S(1)}, s32[512]{0:T(512)}, u32[]{:S(2)}) copy-start(s32[512]{0:T(512)} %param.8) | copy-start | bytes 6148
  2.0 1.1 %copy-start = (bf16[256,3,512]{2,0,1:T(8,128)(2,1)S(1)}, bf16[256,3,512]{2,0,1:T(8,128)(2,1)}, u32[]{:S(2)}) copy-start(bf16[256,3,512]{2,0,1:T(8,128)(2,1)} %param.7) | copy-start | bytes 2359300
  3.1 0.9 %copy-start.1 = (bf16[256,512]{1,0:T(8,128)(2,1)S(1)}, bf16[256,512]{1,0:T(8,128)(2,1)}, u32[]{:S(2)}) copy-start(bf16[256,512]{1,0:T(8,128)(2,1)} %constant.11.clone.inv_lo) | copy-start | bytes 786436
  4.0 0.9 %copy-start.2 = (bf16[256,512]{1,0:T(8,128)(2,1)S(1)}, bf16[256,512]{1,0:T(8,128)(2,1)}, u32[]{:S(2)}) copy-start(bf16[256,512]{1,0:T(8,128)(2,1)} %constant.10.clone.inv_hi) | copy-start | bytes 786436
  5.0 0.9 %copy-start.3 = (bf16[512,256]{1,0:T(8,128)(2,1)S(1)}, bf16[512,256]{1,0:T(8,128)(2,1)}, u32[]{:S(2)}) copy-start(bf16[512,256]{1,0:T(8,128)(2,1)} %constant.9.clone.fwd_lo) | copy-start | bytes 786436
  5.9 0.9 %copy-start.4 = (bf16[512,256]{1,0:T(8,128)(2,1)S(1)}, bf16[512,256]{1,0:T(8,128)(2,1)}, u32[]{:S(2)}) copy-start(bf16[512,256]{1,0:T(8,128)(2,1)} %constant.8.clone.fwd_hi) | copy-start | bytes 786436

commit v3 on v2

v3 whole, which is shorter than its diff:
```python
import functools
import math

import jax
import jax.numpy as jnp
import numpy as np
from jax import lax
from jax.experimental import pallas as pl
from jax.experimental.pallas import tpu as pltpu
from jax.sharding import PartitionSpec as P

LAGS = 256
CHUNKS = 4
MESH = pl.DeviceIdType.MESH


def split_bf16(table):
    high = table.astype(np.float32).astype(jnp.bfloat16)
    low = (table - high.astype(np.float64)).astype(np.float32).astype(jnp.bfloat16)
    return high, low


@functools.lru_cache
def tables(frame_count, count):
    length = 2 * frame_count
    bins = np.arange(frame_count, dtype=np.int64)[:, None]
    own = np.arange(frame_count, dtype=np.int64)[None, :]
    angle = (((2 * bins + 1) * own) % (2 * length)) * (math.pi / length)
    forward = np.concatenate([np.cos(angle), np.sin(angle)], 0)
    per = LAGS // count
    lags = np.arange(LAGS, dtype=np.int64).reshape(count // 4, 2, 2, per)
    lags = lags.transpose(2, 0, 1, 3).reshape(LAGS, 1)
    angle = (((2 * bins.T + 1) * lags) % (2 * length)) * (math.pi / length)
    inverse = np.concatenate([np.cos(angle), -np.sin(angle)], 1) * (2.0 / length)
    return split_bf16(forward) + split_bf16(inverse)


def dot(a, b):
    return jnp.dot(a, b, preferred_element_type=jnp.float32)


def kernel(
    n, groups,
    valid_ref, vel_hbm, mask_ref, fwd_hi_hbm, fwd_lo_hbm, inv_hi_hbm, inv_lo_hbm,
    corr_ref, avg_ref,
    vel_ref, fwd_hi, fwd_lo, inv_hi, inv_lo,
    nxt, spec, part, pair_in, q_ref, z_in, r_ref, x_in, comp_out, comp_in,
    load_s, halo_s, halo_r, pair_s, pair_r, z_s, z_r, x_s, x_r, comp_s, comp_r,
):
    xyz, frames, atoms = vel_ref.shape
    width = atoms // CHUNKS
    nz = n // 4
    per = LAGS // n
    me = lax.axis_index("tm")
    mine = lax.axis_index("comp")
    core = lax.rem(me, 2)
    xpos = lax.rem(me // 2, 2)
    zpos = me // 4
    pair = me + 1 - 2 * core
    across = me + 2 - 4 * xpos
    left = lax.rem(me + n - 1, n)
    right = lax.rem(me + 1, n)

    loads = [
        pltpu.make_async_copy(src, dst, load_s.at[i])
        for i, (src, dst) in enumerate(
            [
                (fwd_hi_hbm, fwd_hi), (fwd_lo_hbm, fwd_lo), (vel_hbm, vel_ref),
                (inv_hi_hbm, inv_hi), (inv_lo_hbm, inv_lo),
            ]
        )
    ]
    for load in loads:
        load.start()

    def along_z(d):
        return lax.rem(zpos + d, nz)

    def z_device(d):
        return along_z(d) * 4 + lax.rem(me, 4)

    def group(d):
        return lax.rem(mine + d, groups)

    barrier = pltpu.get_barrier_semaphore()
    for device in [left, right, pair, across] + [z_device(d) for d in range(1, nz)]:
        pl.semaphore_signal(barrier, inc=1, device_id={"tm": device}, device_id_type=MESH)
    for d in range(1, groups):
        for device in (me, across):
            pl.semaphore_signal(
                barrier, inc=1, device_id={"comp": group(d), "tm": device}, device_id_type=MESH
            )
    pl.semaphore_wait(barrier, 4 + (nz - 1) + 2 * (groups - 1))

    def remote(src, dst, send, recv, device):
        return pltpu.make_async_remote_copy(
            src_ref=src, dst_ref=dst, send_sem=send, recv_sem=recv,
            device_id=device, device_id_type=MESH,
        )

    def halo(c, k):
        lanes = pl.ds(c * width, width)
        return remote(
            vel_hbm.at[k, :, lanes], nxt.at[c, k], halo_s.at[c, k], halo_r.at[c, k], {"tm": left}
        )

    @pl.when(me > 0)
    def _():
        for c in range(CHUNKS):
            for k in range(xyz):
                halo(c, k).start()

    @pl.when(me == n - 1)
    def _():
        nxt[...] = jnp.zeros_like(nxt)

    last_valid = valid_ref[0]

    def keep(offset, lanes):
        row = lax.broadcasted_iota(jnp.int32, (frames, lanes), 0) + (me * frames + offset)
        return jnp.where(row < last_valid, 1.0, 0.0).astype(jnp.bfloat16)

    bins = lax.broadcasted_iota(jnp.int32, (frames, width), 0)
    sign = jnp.where(lax.rem(bins, 2) == 0, 1.0, -1.0)
    weight = mask_ref[...].astype(jnp.float32)

    def spectrum(x):
        return dot(fwd_hi[...], x) + dot(fwd_lo[...], x)

    for load in loads[:3]:
        load.wait()
    step = 2 if CHUNKS % 2 == 0 else 1
    keep_own = keep(0, step * width)
    for c in range(0, CHUNKS, step):
        for k in range(xyz):
            both = spectrum(vel_ref[k, :, c * width : (c + step) * width] * keep_own)
            for j in range(step):
                spec[c + j, k] = both[:, j * width : (j + 1) * width]
    for load in loads[3:]:
        load.wait()

    keep_nxt = keep(frames, width)

    def pair_copy(c):
        return remote(part.at[c, 1 - core], pair_in.at[c], pair_s.at[c], pair_r.at[c], {"tm": pair})

    def z_copy(c, d):
        return remote(
            q_ref.at[c, along_z(d)], z_in.at[c, d - 1], z_s.at[c, d - 1], z_r.at[c, d - 1],
            {"tm": z_device(d)},
        )

    def x_copy(c):
        return remote(r_ref.at[c, 1 - xpos], x_in.at[c], x_s.at[c], x_r.at[c], {"tm": across})

    def lanes_of(c):
        return slice(c * width, (c + 1) * width)

    def atom_sum(c, rows):
        return jnp.sum(weight[:, lanes_of(c)] * rows, axis=1, keepdims=True)

    def after_pair(c):
        pair_copy(c).wait_recv()
        q_ref[c] = part[c, core] + pair_in[c]
        for d in range(1, nz):
            z_copy(c, d).start()

    totals = {}

    def after_z(c):
        rows = q_ref[c, zpos]
        for d in range(1, nz):
            z_copy(c, d).wait_recv()
            rows = rows + z_in[c, d - 1]
        r_ref[c] = rows
        x_copy(c).start()
        totals[c] = (atom_sum(c, r_ref[c, xpos]), atom_sum(c, r_ref[c, 1 - xpos]))

    def correlate(c):
        real = imag = 0.0
        for k in range(xyz):
            if k == 1 and c >= 1:
                after_pair(c - 1)
            if k == xyz - 1 and c >= 2:
                after_z(c - 2)

            @pl.when(me < n - 1)
            def _():
                halo(c, k).wait_recv()

            other = spectrum(nxt[c, k] * keep_nxt)
            nc, ns = -sign * other[frames:], sign * other[:frames]
            ac, as_ = spec[c, k, :frames], spec[c, k, frames:]
            real = real + ac * (ac + nc) + as_ * (as_ + ns)
            imag = imag + as_ * nc - ac * ns
        power = jnp.concatenate([real, imag], 0)
        high = power.astype(jnp.bfloat16)
        low = (power - high.astype(jnp.float32)).astype(jnp.bfloat16)
        sums = dot(inv_hi[...], high) + (dot(inv_hi[...], low) + dot(inv_lo[...], high))
        part[c] = sums.reshape(part.shape[1:])
        pair_copy(c).start()

    for c in range(CHUNKS):
        correlate(c)
    after_pair(CHUNKS - 1)
    if CHUNKS > 1:
        after_z(CHUNKS - 2)
    after_z(CHUNKS - 1)

    total = sum(t[0] for t in totals.values())
    beside = sum(t[1] for t in totals.values())
    real_atoms = jnp.sum(weight, axis=1, keepdims=True)
    comp_out[0, :per] = jnp.broadcast_to(total, (per, 128))
    comp_out[0, per:] = jnp.broadcast_to(real_atoms, (8, 128))
    comp_out[1, :per] = jnp.broadcast_to(beside, (per, 128))
    comp_out[1, per:] = jnp.zeros((8, 128), jnp.float32)

    def comp_copy(side, d):
        return remote(
            comp_out.at[side], comp_in.at[side, d - 1], comp_s.at[side, d - 1],
            comp_r.at[side, d - 1], {"comp": group(d), "tm": (me, across)[side]},
        )

    for side in range(2):
        for d in range(1, groups):
            comp_copy(side, d).start()

    lag = me * per + lax.broadcasted_iota(jnp.int32, (per, width), 0)
    anchors = (last_valid - lag).astype(jnp.float32)
    for c in range(CHUNKS):
        kept = r_ref[c, xpos]
        x_copy(c).wait_recv()
        arrived = x_in[c]
        corr_ref[:, lanes_of(c)] = weight[:, lanes_of(c)] * (kept + arrived) / anchors
        total = total + atom_sum(c, arrived)
    sums = jnp.broadcast_to(total, (per, 128))
    count = jnp.broadcast_to(real_atoms, (8, 128))
    for side in range(2):
        for d in range(1, groups):
            comp_copy(side, d).wait_recv()
            sums = sums + comp_in[side, d - 1, :per]
            count = count + comp_in[side, d - 1, per:]
    avg_ref[...] = sums / anchors[:, :128] / jnp.maximum(count[:1], 1.0)

    @pl.when(me > 0)
    def _():
        for c in range(CHUNKS):
            for k in range(xyz):
                halo(c, k).wait_send()

    for c in range(CHUNKS):
        pair_copy(c).wait_send()
        x_copy(c).wait_send()
        for d in range(1, nz):
            z_copy(c, d).wait_send()
    for side in range(2):
        for d in range(1, groups):
            comp_copy(side, d).wait_send()


def body(velocities, atom_mask, valid_frames):
    frames, xyz, atoms = velocities.shape
    n = lax.axis_size("tm")
    groups = lax.axis_size("comp")
    nz, per, width = n // 4, LAGS // n, atoms // CHUNKS
    f32, bf16 = jnp.float32, jnp.bfloat16
    vmem = pl.BlockSpec(memory_space=pltpu.VMEM)
    hbm = pl.BlockSpec(memory_space=pltpu.HBM)
    dma = pltpu.SemaphoreType.DMA
    correlation, average = pl.pallas_call(
        functools.partial(kernel, n, groups),
        out_shape=(
            jax.ShapeDtypeStruct((per, atoms), f32),
            jax.ShapeDtypeStruct((per, 128), f32),
        ),
        in_specs=[pl.BlockSpec(memory_space=pltpu.SMEM), hbm, vmem] + [hbm] * 4,
        out_specs=(vmem, vmem),
        scratch_shapes=[
            pltpu.VMEM((xyz, frames, atoms), bf16),
            pltpu.VMEM((2 * frames, frames), bf16),
            pltpu.VMEM((2 * frames, frames), bf16),
            pltpu.VMEM((LAGS, 2 * frames), bf16),
            pltpu.VMEM((LAGS, 2 * frames), bf16),
            pltpu.VMEM((CHUNKS, xyz, frames, width), bf16),
            pltpu.VMEM((CHUNKS, xyz, 2 * frames, width), f32),
            pltpu.VMEM((CHUNKS, 2, nz, 2, per, width), f32),
            pltpu.VMEM((CHUNKS, nz, 2, per, width), f32),
            pltpu.VMEM((CHUNKS, nz, 2, per, width), f32),
            pltpu.VMEM((CHUNKS, nz - 1, 2, per, width), f32),
            pltpu.VMEM((CHUNKS, 2, per, width), f32),
            pltpu.VMEM((CHUNKS, per, width), f32),
            pltpu.VMEM((2, per + 8, 128), f32),
            pltpu.VMEM((2, groups - 1, per + 8, 128), f32),
            dma((5,)),
            dma((CHUNKS, xyz)), dma((CHUNKS, xyz)),
            dma((CHUNKS,)), dma((CHUNKS,)),
            dma((CHUNKS, nz - 1)), dma((CHUNKS, nz - 1)),
            dma((CHUNKS,)), dma((CHUNKS,)),
            dma((2, groups - 1)), dma((2, groups - 1)),
        ],
        compiler_params=pltpu.CompilerParams(
            collective_id=0, has_side_effects=True, vmem_limit_bytes=63 * 1024 * 1024
        ),
    )(
        valid_frames, jnp.transpose(velocities, (1, 0, 2)), atom_mask[None, :],
        *tables(frames, n),
    )
    return correlation, average[:, 0]


def solution(mesh):
    return jax.shard_map(
        body,
        mesh=mesh,
        in_specs=(P("tm", None, "comp"), P("comp"), P()),
        out_specs=(P("tm", "comp"), P("tm")),
        check_vma=False,
    )
```

time: 36.4 us -> 34.7 us (0.953)
  local copies, waits for them, and re-layouts: 6.85 us -> 2.7 us
  Pallas kernels: 27.9 us -> 30.4 us
    unnamed x13 -> x1, local copies, waits for them, and re-layouts: 6.22 us -> 1.37 us
    pallas_call x1, Pallas kernels: 27.9 us -> 30.4 us  [body(): pl.pallas_call(functools.partial(kernel, n, groups), out_shape=(jax.Shape...]
    slice x1, local copies, waits for them, and re-layouts: 0.63 us -> 1.32 us  [body(): return (correlation, average[:, 0])]
where the time goes in v3:
time: 34.7 us; the launch traced here: 34.4 us
  Pallas kernels  30.4 us (88%)
  local copies, waits for them, and re-layouts  2.7 us (8%)
  between operations  1.29 us (4%)
    pallas_call x1, Pallas kernels, body(): pl.pallas_call(functools.partial(kernel, n, groups), out_shape=(jax.Shape...  30.4 us
    unnamed x1, local copies, waits for them, and re-layouts  1.37 us
    slice x1, local copies, waits for them, and re-layouts, body(): return (correlation, average[:, 0])  1.32 us

profile of v3, /device:TPU:0, one launch (start us, length us, event | category | flops | bytes accessed | tf_op | source)
XLA Modules:
  0.0 34.4 jit_solution(5907157388596556576)
XLA Ops:
  1.3 30.4 %shard_map.86 = (f32[16,512]{1,0:T(8,128)}, f32[16,128]{1,0:T(8,128)}) custom-call(s32[1]{0:T(128)S(6)} %copy.10.valid_ref, bf16[3,256,512]{2,1,0:T(8,128)(2,1)} %bitcast.2, s32[1,512]{1,0:T(1,128)} %bitcast.3, bf16[512,256]{1,0:T(8,128)(2,1)} %constant.8.clone.fwd_hi_hbm, bf16[512,256]{1,0:T(8,128)(2,1)} %constant.9.clone.fwd_lo_hbm, ...), custom_call_target="tpu_custom_call" | custom-call | tf_op jit(solution)/shard_map/pallas_call | solution.py:270
  31.7 1.3 %slice_reduce_fusion = f32[16]{0:T(128)} fusion(f32[16,128]{1,0:T(8,128)} %get-tuple-element.5), kind=kLoop, calls=%fused_computation | loop fusion | bytes 128 | tf_op jit(solution)/shard_map/slice | solution.py:308
  33.0 1.4 %copy.11 = f32[16,512]{1,0:T(8,128)} copy(f32[16,512]{1,0:T(8,128)} %get-tuple-element.8) | data formatting | bytes 65536

commit v4 on v3

--- a/solution.py
+++ b/solution.py
@@ -10,7 +10,7 @@
 from jax.sharding import PartitionSpec as P
 
 LAGS = 256
-CHUNKS = 4
+CHUNKS = 2
 MESH = pl.DeviceIdType.MESH
 
 
@@ -299,7 +299,7 @@
             dma((2, groups - 1)), dma((2, groups - 1)),
         ],
         compiler_params=pltpu.CompilerParams(
-            collective_id=0, has_side_effects=True, vmem_limit_bytes=63 * 1024 * 1024
+            collective_id=0, has_side_effects=True, vmem_limit_bytes=56_500_000
         ),
     )(
         valid_frames, jnp.transpose(velocities, (1, 0, 2)), atom_mask[None, :],

time: 34.7 us -> 30 us (0.86)
  Pallas kernels: 30.4 us -> 26.6 us
  local copies, waits for them, and re-layouts: 2.7 us -> 1.91 us
    pallas_call x1, Pallas kernels: 30.4 us -> 26.6 us  [body(): pl.pallas_call(functools.partial(kernel, n, groups), out_shape=(jax.Shape...]
    slice x1, local copies, waits for them, and re-layouts: 1.32 us -> 0.63 us  [body(): return (correlation, average[:, 0])]
    unnamed x1 -> x3, local copies, waits for them, and re-layouts: 1.37 us -> 1.29 us
where the time goes in v4:
time: 30 us; the launch traced here: 29.8 us
  Pallas kernels  26.6 us (89%)
  local copies, waits for them, and re-layouts  1.91 us (6%)
  between operations  1.29 us (4%)
    pallas_call x1, Pallas kernels, body(): pl.pallas_call(functools.partial(kernel, n, groups), out_shape=(jax.Shape...  26.6 us
    unnamed x3, local copies, waits for them, and re-layouts  1.29 us
    slice x1, local copies, waits for them, and re-layouts, body(): return (correlation, average[:, 0])  0.63 us

profile of v4, /device:TPU:0, one launch (start us, length us, event | category | flops | bytes accessed | tf_op | source)
XLA Modules:
  0.0 29.8 jit_solution(1566221932224565777)
XLA Ops:
  1.3 0.0 copy-start
  1.3 0.7 %copy-done = s32[512]{0:T(512)S(1)} copy-done((s32[512]{0:T(512)S(1)}, s32[512]{0:T(512)}, u32[]{:S(2)}) %copy-start) | copy-done | bytes 2072
  2.0 26.6 %shard_map.86 = (f32[16,512]{1,0:T(8,128)S(1)}, f32[16,128]{1,0:T(8,128)S(1)}) custom-call(s32[1]{0:T(128)S(6)} %copy.10.valid_ref, bf16[3,256,512]{2,1,0:T(8,128)(2,1)} %bitcast.3, s32[1,512]{1,0:T(1,128)S(1)} %bitcast.2, bf16[512,256]{1,0:T(8,128)(2,1)} %constant.8.clone.fwd_hi_hbm, bf16[512,256]{1,0:T(8,128)(2,1)} %constant.9.clone.fwd_lo_hbm, ...), custom_call_target="tpu_custom_call" | custom-call | tf_op jit(solution)/shard_map/pallas_call | solution.py:270
  28.5 0.6 %slice_reduce_fusion = f32[16]{0:T(128)} fusion(f32[16,128]{1,0:T(8,128)S(1)} %get-tuple-element.5), kind=kLoop, calls=%fused_computation | loop fusion | bytes 128 | tf_op jit(solution)/shard_map/slice | solution.py:308
  29.2 0.6 %copy.11 = f32[16,512]{1,0:T(8,128)} copy(f32[16,512]{1,0:T(8,128)S(1)} %get-tuple-element.8) | data formatting | bytes 65536
Async XLA Ops:
  1.3 0.7 %copy-start = (s32[512]{0:T(512)S(1)}, s32[512]{0:T(512)}, u32[]{:S(2)}) copy-start(s32[512]{0:T(512)} %param.8) | copy-start | bytes 6148

commit v5 on v4

--- a/solution.py
+++ b/solution.py
@@ -41,9 +41,9 @@
 
 def kernel(
     n, groups,
-    valid_ref, vel_hbm, mask_ref, fwd_hi_hbm, fwd_lo_hbm, inv_hi_hbm, inv_lo_hbm,
+    valid_ref, vel_hbm, mask_hbm, fwd_hi_hbm, fwd_lo_hbm, inv_hi_hbm, inv_lo_hbm,
     corr_ref, avg_ref,
-    vel_ref, fwd_hi, fwd_lo, inv_hi, inv_lo,
+    vel_ref, mask_ref, fwd_hi, fwd_lo, inv_hi, inv_lo,
     nxt, spec, part, pair_in, q_ref, z_in, r_ref, x_in, comp_out, comp_in,
     load_s, halo_s, halo_r, pair_s, pair_r, z_s, z_r, x_s, x_r, comp_s, comp_r,
 ):
@@ -66,7 +66,7 @@
         for i, (src, dst) in enumerate(
             [
                 (fwd_hi_hbm, fwd_hi), (fwd_lo_hbm, fwd_lo), (vel_hbm, vel_ref),
-                (inv_hi_hbm, inv_hi), (inv_lo_hbm, inv_lo),
+                (inv_hi_hbm, inv_hi), (inv_lo_hbm, inv_lo), (mask_hbm, mask_ref),
             ]
         )
     ]
@@ -122,7 +122,6 @@
 
     bins = lax.broadcasted_iota(jnp.int32, (frames, width), 0)
     sign = jnp.where(lax.rem(bins, 2) == 0, 1.0, -1.0)
-    weight = mask_ref[...].astype(jnp.float32)
 
     def spectrum(x):
         return dot(fwd_hi[...], x) + dot(fwd_lo[...], x)
@@ -138,6 +137,7 @@
                 spec[c + j, k] = both[:, j * width : (j + 1) * width]
     for load in loads[3:]:
         load.wait()
+    weight = mask_ref[...].astype(jnp.float32)
 
     keep_nxt = keep(frames, width)
 
@@ -273,10 +273,11 @@
             jax.ShapeDtypeStruct((per, atoms), f32),
             jax.ShapeDtypeStruct((per, 128), f32),
         ),
-        in_specs=[pl.BlockSpec(memory_space=pltpu.SMEM), hbm, vmem] + [hbm] * 4,
+        in_specs=[pl.BlockSpec(memory_space=pltpu.SMEM)] + [hbm] * 6,
         out_specs=(vmem, vmem),
         scratch_shapes=[
             pltpu.VMEM((xyz, frames, atoms), bf16),
+            pltpu.VMEM((1, atoms), jnp.int32),
             pltpu.VMEM((2 * frames, frames), bf16),
             pltpu.VMEM((2 * frames, frames), bf16),
             pltpu.VMEM((LAGS, 2 * frames), bf16),
@@ -291,7 +292,7 @@
             pltpu.VMEM((CHUNKS, per, width), f32),
             pltpu.VMEM((2, per + 8, 128), f32),
             pltpu.VMEM((2, groups - 1, per + 8, 128), f32),
-            dma((5,)),
+            dma((6,)),
             dma((CHUNKS, xyz)), dma((CHUNKS, xyz)),
             dma((CHUNKS,)), dma((CHUNKS,)),
             dma((CHUNKS, nz - 1)), dma((CHUNKS, nz - 1)),

time: 30 us -> 30 us (level)
  no operation moved by 1% of the time
where the time goes in v5:
time: 30 us; the launch traced here: 29.8 us
  Pallas kernels  26.6 us (89%)
  local copies, waits for them, and re-layouts  1.91 us (6%)
  between operations  1.29 us (4%)
    pallas_call x1, Pallas kernels, body(): pl.pallas_call(functools.partial(kernel, n, groups), out_shape=(jax.Shape...  26.6 us
    unnamed x3, local copies, waits for them, and re-layouts  1.29 us
    slice x1, local copies, waits for them, and re-layouts, body(): return (correlation, average[:, 0])  0.63 us

profile of v5, /device:TPU:0, one launch (start us, length us, event | category | flops | bytes accessed | tf_op | source)
XLA Modules:
  0.0 29.8 jit_solution(8661826026386956293)
XLA Ops:
  1.3 0.0 copy-start
  1.3 0.7 %copy-done = s32[512]{0:T(512)S(1)} copy-done((s32[512]{0:T(512)S(1)}, s32[512]{0:T(512)}, u32[]{:S(2)}) %copy-start) | copy-done | bytes 2072
  2.0 26.6 %shard_map.86 = (f32[16,512]{1,0:T(8,128)S(1)}, f32[16,128]{1,0:T(8,128)S(1)}) custom-call(s32[1]{0:T(128)S(6)} %copy.10.valid_ref, bf16[3,256,512]{2,1,0:T(8,128)(2,1)} %bitcast.3, s32[1,512]{1,0:T(1,128)S(1)} %bitcast.2, bf16[512,256]{1,0:T(8,128)(2,1)} %constant.8.clone.fwd_hi_hbm, bf16[512,256]{1,0:T(8,128)(2,1)} %constant.9.clone.fwd_lo_hbm, ...), custom_call_target="tpu_custom_call" | custom-call | tf_op jit(solution)/shard_map/pallas_call | solution.py:270
  28.6 0.6 %slice_reduce_fusion = f32[16]{0:T(128)} fusion(f32[16,128]{1,0:T(8,128)S(1)} %get-tuple-element.5), kind=kLoop, calls=%fused_computation | loop fusion | bytes 128 | tf_op jit(solution)/shard_map/slice | solution.py:309
  29.2 0.6 %copy.11 = f32[16,512]{1,0:T(8,128)} copy(f32[16,512]{1,0:T(8,128)S(1)} %get-tuple-element.8) | data formatting | bytes 65536
Async XLA Ops:
  1.3 0.7 %copy-start = (s32[512]{0:T(512)S(1)}, s32[512]{0:T(512)}, u32[]{:S(2)}) copy-start(s32[512]{0:T(512)} %param.8) | copy-start | bytes 6148
